TPU v7x, 128 devices: a whole 4x4x4 slice. The times are simulated.
128 devices in a mesh: parts: 128 (over y, z, x, core).
Axes of the slice: x: 4, y: 4, z: 4, core: 2. Of those that a mesh axis runs over, the one named last changes fastest.
Arguments:
- a_cols: int32 [4096, 7], replicated, may hold values from 0 to 4095, as said below
- p_col: int32 [4096], replicated, may hold values from 0 to 255, as said below
- coarse_cols: int32 [256, 14], replicated, may hold values from 0 to 255, as said below
- a_vals: bfloat16 [4096, 7, 192, 192], P('parts'), may hold values from -0.15625 to 0.15625
- p_vals: bfloat16 [4096, 192, 192], P('parts'), may hold values from -0.5 to 0.5
Outputs:
- coarse: float32 [256, 14, 192, 192], P('parts')
Inputs may be any that keep to these rules, and one draw needn't show every extreme that they name: `a_cols`: regions are numbered 0 to 127; fine row i lies in region g = i // 32 with local index l = i % 32; o is the list 0, 1, -1, 4, -4, 16, -16 and region g + o(s) is taken cyclically. Slot 0 of row i holds i. For l < 6, slot l + 1 holds the row of region g + o(l + 1) whose local index is q - 1, where q is the slot whose offset is the negative of o(l + 1), and the other slots hold rows of region g with local index 6 or more. For l >= 6 slots 1 to 6 hold rows of region g. For fine row i of region g with local index l: if l < 6, p_col[i] is a coarse row of region g + o(l + 1), else of region g; coarse row r belongs to region r // 2. `coarse_cols`: row r of region g lists, in an order of its own, the 2 coarse rows of each of the regions g + o(s), s = 0 to 6.
All inputs are finite; a program needn't handle non-finite values.
Results may differ from a plain program's by a relative error of at most 0.0029.
Values may be sent and summed in bfloat16 or wider, within the bound.
No kernel may reach another device: no remote copies, remote signals or barrier semaphores. Data moves between devices by JAX's collectives and lax.ppermute only.
A program may use at most 256 MiB of HBM per device.

v0:
```python
import jax
import jax.numpy as jnp
from jax import lax
from jax.sharding import PartitionSpec as P

OFFSETS = [0, 1, -1, 4, -4, 16, -16]
OPPOSITE = [0, 2, 1, 4, 3, 6, 5]


def shifted(value, axis, by):
    count = lax.axis_size(axis)
    return lax.ppermute(value, axis, [(i, (i + by) % count) for i in range(count)])


def spread(coarse_ids, targets, galerkin, listed, first_coarse, form):
    coarse_count = listed.shape[0]
    local_coarse = coarse_ids - first_coarse
    hit_row = local_coarse[:, None] == jnp.arange(coarse_count, dtype=jnp.int32)[None, :]
    equal_slots = listed[None, None, :, :] == targets[:, :, None, None]
    first_slot = equal_slots & (jnp.cumsum(equal_slots.astype(jnp.int32), axis=3) == 1)
    weights = (first_slot & hit_row[:, None, :, None]).astype(jnp.float32)
    return jnp.einsum(form, weights, galerkin, precision=lax.Precision.HIGHEST)


def per_device(a_cols, p_col, coarse_cols, a_vals, p_vals):
    row_count = a_vals.shape[0]
    region_count = lax.axis_size("parts")
    region_id = lax.axis_index("parts")
    coarse_count = coarse_cols.shape[0] // region_count
    first_row = region_id * row_count
    first_coarse = region_id * coarse_count
    face_blocks = []
    for face_id in range(1, 7):
        face_blocks.append(shifted(p_vals[face_id - 1], "parts", OFFSETS[face_id]))
    prolong_pool = jnp.concatenate([p_vals, jnp.stack(face_blocks)], axis=0)
    columns = lax.dynamic_slice_in_dim(a_cols, first_row, row_count, 0)
    face_index = row_count + jnp.array(OPPOSITE, dtype=jnp.int32) - 1
    outside = columns // row_count != region_id
    pool_index = jnp.where(outside, face_index[None, :], columns - first_row)
    gathered = prolong_pool[pool_index]
    products = jnp.einsum(
        "ikab,ikbc->ikac", a_vals, gathered, preferred_element_type=jnp.float32
    ).astype(jnp.bfloat16)
    targets = p_col[columns]
    own_coarse = lax.dynamic_slice_in_dim(p_col, first_row, row_count, 0)
    listed = lax.dynamic_slice_in_dim(coarse_cols, first_coarse, coarse_count, 0)
    inner_terms = jnp.einsum(
        "iba,ikbc->iakc", p_vals[6:], products[6:], preferred_element_type=jnp.float32
    )
    accumulated = spread(
        own_coarse[6:], targets[6:], inner_terms, listed, first_coarse, "ikmc,iakb->mcab"
    )
    received = []
    sender_ids = []
    sender_targets = []
    face_terms = jnp.einsum(
        "iba,ikbc->iakc", p_vals[:6], products[:6], preferred_element_type=jnp.float32
    )
    for face_id in range(1, 7):
        received.append(shifted(face_terms[face_id - 1], "parts", OFFSETS[face_id]))
    for face_id in range(1, 7):
        sender = (region_id - OFFSETS[face_id]) % region_count
        sender_row = sender * row_count + face_id - 1
        sender_ids.append(p_col[sender_row])
        sender_targets.append(p_col[a_cols[sender_row]])
    form = "ikmc,iakb->mcab"
    accumulated = accumulated + spread(
        jnp.stack(sender_ids),
        jnp.stack(sender_targets),
        jnp.stack(received),
        listed,
        first_coarse,
        form,
    )
    return accumulated


def solution(mesh):
    placed = (P(), P(), P(), P("parts", None, None, None), P("parts", None, None))
    return jax.shard_map(
        per_device,
        mesh=mesh,
        in_specs=placed,
        out_specs=P("parts", None, None, None),
        check_vma=False,
    )
```

profile of v0, /device:TPU:0, one launch (start us, length us, event | category | flops | bytes accessed | tf_op | source)
XLA Modules:
  0.0 264.8 jit_solution(5245046398668363788)
XLA Ops:
  0.0 2.0 slice_bitcast_fusion.6
  2.0 8.2 %collective-permute-start.1 = (bf16[192,192]{1,0:T(8,128)(2,1)}, bf16[192,192]{1,0:T(8,128)(2,1)}, u32[]{:S(2)}, u32[]{:S(2)}) collective-permute-start(bf16[192,192]{1,0:T(8,128)(2,1)} %get-tuple-element.21), channel_id=1, source_target_pairs={{0,127},{1,0},{2,1},{3,2},{4,3},{5,4},{6,5},{7,6},{8,7},{9,8},{10,... | collective-permute-start | bytes 221192 | tf_op jit(solution)/shard_map/ppermute | solution.py:12
  10.3 7.7 %collective-permute-start.3 = (bf16[192,192]{1,0:T(8,128)(2,1)}, bf16[192,192]{1,0:T(8,128)(2,1)}, u32[]{:S(2)}, u32[]{:S(2)}) collective-permute-start(bf16[192,192]{1,0:T(8,128)(2,1)} %get-tuple-element.19), channel_id=1, source_target_pairs={{0,124},{1,125},{2,126},{3,127},{4,0},{5,1},{6,2},{7,3},{8,4},{9,5... | collective-permute-start | bytes 221192 | tf_op jit(solution)/shard_map/ppermute | solution.py:12
  18.0 3.9 %constant_dynamic-update-slice_fusion = bf16[38,192,192]{2,1,0:T(8,128)(2,1)} fusion(bf16[32,192,192]{2,1,0:T(8,128)(2,1)} %param.10), kind=kLoop, calls=%fused_computation.61 | loop fusion | bytes 5505024
  21.9 1.7 fusion.50
  23.7 0.7 fusion.44
  24.4 1.0 dynamic-slice_reduce_fusion
  25.4 0.8 add_select_fusion.1
  26.5 0.1 reshape.257
  26.6 1.7 gather_fusion
  28.8 0.7 reduce_window_sum.22
  29.6 0.6 iota_compare_fusion.1
  30.2 0.6 gather_fusion.2
  30.9 0.6 gather_fusion.3
  31.5 0.6 gather_fusion.4
  32.2 0.6 gather_fusion.5
  32.8 0.6 gather_fusion.6
  33.5 0.6 gather_fusion.7
  34.2 4.7 %reduce_window_sum.23 = s32[6,7,2,14]{3,1,0,2:T(8,128)} reduce-window(s32[6,7,2,14]{3,1,0,2:T(8,128)S(1)} %compare_convert_fusion.1, s32[]{:T(128)} %constant.101.clone.1), window={size=1x1x1x14 pad=0_0x0_0x0_0x13_0}, to_apply=%region_1.2 | reduce-window | flops 15288 | bytes 9412 | tf_op jit(solution)/shard_map/jit(cumsum)/reduce_window_sum | solution.py:20
  38.9 3.8 %stack.76 = s32[6]{0:T(128)S(1)} concatenate(s32[1]{0:T(128)} %get-tuple-element.29, s32[1]{0:T(128)} %get-tuple-element.28, s32[1]{0:T(128)} %get-tuple-element.27, s32[1]{0:T(128)} %get-tuple-element.26, s32[1]{0:T(128)} %get-tuple-element.30, s32[1]{0:T(128)} %get-tuple-element.25), dimensions={0} | concatenate | bytes 48 | tf_op jit(solution)/shard_map/stack | solution.py:68
  42.8 0.5 iota_compare_fusion
  43.3 5.7 %collective-permute-start.5 = (bf16[192,192]{1,0:T(8,128)(2,1)S(1)}, bf16[192,192]{1,0:T(8,128)(2,1)S(1)}, u32[]{:S(2)}, u32[]{:S(2)}) collective-permute-start(bf16[192,192]{1,0:T(8,128)(2,1)S(1)} %get-tuple-element.17), channel_id=1, source_target_pairs={{0,112},{1,113},{2,114},{3,115},{4,116},{5,117},{6,118},{7,119},{8... | collective-permute-start | bytes 221192 | tf_op jit(solution)/shard_map/ppermute | solution.py:12
  49.0 1.5 bitcast_dynamic-update-slice_fusion.11
  50.6 1.5 bitcast_dynamic-update-slice_fusion.10
  52.1 1.5 bitcast_dynamic-update-slice_fusion.9
  53.7 1.5 bitcast_dynamic-update-slice_fusion.8
  55.2 1.5 bitcast_dynamic-update-slice_fusion.7
  56.7 0.6 bitcast_dynamic-update-slice_fusion.6
  57.4 13.8 %gather_fusion.1 = bf16[224,192,192]{2,1,0:T(8,128)(2,1)} fusion(bf16[38,192,192]{2,1,0:T(8,128)(2,1)} %bitcast_dynamic-update-slice_fusion.6, s32[1024]{0:T(1024)S(1)} %pad_clamp_fusion.6), kind=kCustom, calls=%fused_computation.1 | custom fusion | bytes 33031040 | tf_op jit(solution)/shard_map/gather | solution.py:40
  71.2 24.8 %convolution_convert_fusion = bf16[32,7,192,192]{3,2,1,0:T(8,128)(2,1)} fusion(bf16[32,7,192,192]{3,2,1,0:T(8,128)(2,1)} %bitcast.131, bf16[32,7,192,192]{3,2,1,0:T(8,128)(2,1)} %param.9), kind=kOutput, calls=%fused_computation.14 | convolution fusion | flops 3179151360 | bytes 49545216 | tf_op jit(solution)/shard_map/ikab,ikbc->ikac/dot_general | solution.py:41
  95.9 3.4 %fusion.8 = f32[6,192,7,192]{1,3,2,0:T(8,128)S(1)} fusion(bf16[32,7,192,192]{3,2,1,0:T(8,128)(2,1)} %convolution_convert_fusion, bf16[32,192,192]{2,1,0:T(8,128)(2,1)S(1)} %copy-done.3), kind=kOutput, calls=%fused_computation.18 | convolution fusion | flops 594542592 | bytes 23298048 | tf_op jit(solution)/shard_map/iba,ikbc->iakc/dot_general | solution.py:56
  99.3 3.5 %slice_bitcast_fusion = (f32[192,7,192]{0,2,1:T(8,128)}, f32[192,7,192]{0,2,1:T(8,128)}, f32[192,7,192]{0,2,1:T(8,128)}, f32[192,7,192]{0,2,1:T(8,128)}, f32[192,7,192]{0,2,1:T(8,128)}, /*index=5*/f32[192,7,192]{0,2,1:T(8,128)}) fusion(f32[6,192,7,192]{1,3,2,0:T(8,128)S(1)} %fusion.8), kind=kLoop, calls=%fused_computation.21 | loop fusion | bytes 12386304 | tf_op jit(solution)/shard_map/squeeze | solution.py:60
  102.9 7.2 %collective-permute-start.7 = (f32[192,7,192]{0,2,1:T(8,128)}, f32[192,7,192]{0,2,1:T(8,128)}, u32[]{:S(2)}, u32[]{:S(2)}) collective-permute-start(f32[192,7,192]{0,2,1:T(8,128)} %get-tuple-element.15), channel_id=1, source_target_pairs={{0,127},{1,0},{2,1},{3,2},{4,3},{5,4},{6,5},{7,6},{8,7},{9,8},{10,... | collective-permute-start | bytes 3096584 | tf_op jit(solution)/shard_map/ppermute | solution.py:12
  110.0 7.7 %collective-permute-start.9 = (f32[192,7,192]{0,2,1:T(8,128)}, f32[192,7,192]{0,2,1:T(8,128)}, u32[]{:S(2)}, u32[]{:S(2)}) collective-permute-start(f32[192,7,192]{0,2,1:T(8,128)} %get-tuple-element.13), channel_id=1, source_target_pairs={{0,124},{1,125},{2,126},{3,127},{4,0},{5,1},{6,2},{7,3},{8,4},{9,5... | collective-permute-start | bytes 3096584 | tf_op jit(solution)/shard_map/ppermute | solution.py:12
  117.8 18.0 %fusion.4 = f32[26,7,192,192]{3,2,1,0:T(8,128)} fusion(bf16[32,7,192,192]{3,2,1,0:T(8,128)(2,1)} %convolution_convert_fusion, bf16[26,192,192,1]{2,1,3,0:T(8,128)(2,1)S(1)} %copy-done.4), kind=kOutput, calls=%fused_computation.12 | convolution fusion | flops 2576351232 | bytes 45268992 | tf_op jit(solution)/shard_map/iba,ikbc->iakc/dot_general | solution.py:47
  135.8 46.3 %copy.22 = f32[26,7,192,192]{2,0,1,3:T(8,128)} copy(f32[26,7,192,192]{3,2,1,0:T(8,128)} %fusion.4) | data formatting | bytes 53673984 | tf_op jit(solution)/shard_map/iba,ikbc->iakc/dot_general | solution.py:47
  182.1 26.5 %fusion = f32[2,14,192,192,1]{3,1,4,2,0:T(8,128)} fusion(f32[26,7,192,192]{2,0,1,3:T(8,128)} %copy.22, s32[26,7,2,14]{0,3,1,2:T(8,128)S(1)} %copy-done.6, s32[26,7]{0,1:T(8,128)S(1)} %copy-done.11, s32[2,14]{1,0:T(2,128)S(1)} %copy-done.13, pred[26,2]{0,1:T(4,128)(4,1)S(1)} %copy-done.14), kind=kOutput, calls=%fused_computation.8 | convolution fusion | flops 2254327808 | bytes 30987036 | tf_op jit(solution)/shard_map/ikmc,iakb->mcab/dot_general | solution.py:22
  208.6 5.6 %collective-permute-start.11 = (f32[192,7,192]{0,2,1:T(8,128)S(1)}, f32[192,7,192]{0,2,1:T(8,128)S(1)}, u32[]{:S(2)}, u32[]{:S(2)}) collective-permute-start(f32[192,7,192]{0,2,1:T(8,128)S(1)} %copy-done.5), channel_id=1, source_target_pairs={{0,112},{1,113},{2,114},{3,115},{4,116},{5,117},{6,118},{7,119},{8... | collective-permute-start | bytes 3096584 | tf_op jit(solution)/shard_map/ppermute | solution.py:12
  214.2 2.6 bitcast_dynamic-update-slice_fusion.5
  216.8 2.5 bitcast_dynamic-update-slice_fusion.4
  219.4 2.6 bitcast_dynamic-update-slice_fusion.3
  222.0 2.5 bitcast_dynamic-update-slice_fusion.2
  224.6 2.6 bitcast_dynamic-update-slice_fusion.1
  227.1 9.2 %collective-permute-done.11 = f32[192,7,192]{0,2,1:T(8,128)S(1)} collective-permute-done((f32[192,7,192]{0,2,1:T(8,128)S(1)}, f32[192,7,192]{0,2,1:T(8,128)S(1)}, u32[]{:S(2)}, u32[]{:S(2)}) %collective-permute-start.11) | collective-permute-done | bytes 1032224 | tf_op jit(solution)/shard_map/ppermute | solution.py:12
  236.3 1.2 bitcast_dynamic-update-slice_fusion
  237.5 10.1 %copy.18 = f32[6,192,7,192]{3,2,0,1:T(8,128)} copy(f32[6,192,7,192]{1,3,2,0:T(8,128)} %bitcast_dynamic-update-slice_fusion) | data formatting | bytes 12386304 | tf_op jit(solution)/shard_map/stack | solution.py:70
  247.6 11.5 %bitcast_add_fusion = f32[2,14,192,192]{3,1,2,0:T(8,128)S(1)} fusion(f32[2,14,192,192,1]{3,1,4,2,0:T(8,128)} %fusion, f32[6,192,7,192]{3,2,0,1:T(8,128)} %copy.18, s32[6,7,2,14]{3,1,0,2:T(8,128)S(1)} %copy-done.7, s32[6,7]{1,0:T(8,128)S(1)} %copy-done.9, s32[2,14]{1,0:T(2,128)S(1)} %copy-done.13, pred[6,2]{0,1:T(4,128)(4,1)S(1)} %copy-done.15), kind=kOutput, calls=%fused_computation.17 | convolution fusion | flops 521261664 | bytes 14455684 | tf_op jit(solution)/shard_map/ikmc,iakb->mcab/dot_general | solution.py:22
  259.2 5.6 %copy.19 = f32[2,14,192,192]{3,2,1,0:T(8,128)} copy(f32[2,14,192,192]{3,1,2,0:T(8,128)S(1)} %bitcast_add_fusion) | data formatting | bytes 8257536 | tf_op jit(solution)/shard_map/add | solution.py:67
  (76 shorter events, 1.2 us)
Async XLA Ops:
  0.0 28.6 %copy-start = (s32[256,14]{0,1:T(8,128)S(1)}, s32[256,14]{0,1:T(8,128)}, u32[]{:S(2)}) copy-start(s32[256,14]{0,1:T(8,128)} %param.8) | copy-start | bytes 43012
  0.0 21.9 %copy-start.3 = (bf16[32,192,192]{2,1,0:T(8,128)(2,1)S(1)}, bf16[32,192,192]{2,1,0:T(8,128)(2,1)}, u32[]{:S(2)}) copy-start(bf16[32,192,192]{2,1,0:T(8,128)(2,1)} %param.10) | copy-start | bytes 7077892
  2.0 41.3 %collective-permute-start = (bf16[192,192]{1,0:T(8,128)(2,1)}, bf16[192,192]{1,0:T(8,128)(2,1)}, u32[]{:S(2)}, u32[]{:S(2)}) collective-permute-start(bf16[192,192]{1,0:T(8,128)(2,1)} %get-tuple-element.22), channel_id=1, source_target_pairs={{0,1},{1,2},{2,3},{3,4},{4,5},{5,6},{6,7},{7,8},{8,9},{9,10},{10,1... | collective-permute-start | bytes 221192 | tf_op jit(solution)/shard_map/ppermute | solution.py:12
  2.0 48.5 %collective-permute-start.1 = (bf16[192,192]{1,0:T(8,128)(2,1)}, bf16[192,192]{1,0:T(8,128)(2,1)}, u32[]{:S(2)}, u32[]{:S(2)}) collective-permute-start(bf16[192,192]{1,0:T(8,128)(2,1)} %get-tuple-element.21), channel_id=1, source_target_pairs={{0,127},{1,0},{2,1},{3,2},{4,3},{5,4},{6,5},{7,6},{8,7},{9,8},{10,... | collective-permute-start | bytes 221192 | tf_op jit(solution)/shard_map/ppermute | solution.py:12
  10.3 41.8 %collective-permute-start.2 = (bf16[192,192]{1,0:T(8,128)(2,1)}, bf16[192,192]{1,0:T(8,128)(2,1)}, u32[]{:S(2)}, u32[]{:S(2)}) collective-permute-start(bf16[192,192]{1,0:T(8,128)(2,1)} %get-tuple-element.20), channel_id=1, source_target_pairs={{0,4},{1,5},{2,6},{3,7},{4,8},{5,9},{6,10},{7,11},{8,12},{9,13},{1... | collective-permute-start | bytes 221192 | tf_op jit(solution)/shard_map/ppermute | solution.py:12
  10.3 43.4 %collective-permute-start.3 = (bf16[192,192]{1,0:T(8,128)(2,1)}, bf16[192,192]{1,0:T(8,128)(2,1)}, u32[]{:S(2)}, u32[]{:S(2)}) collective-permute-start(bf16[192,192]{1,0:T(8,128)(2,1)} %get-tuple-element.19), channel_id=1, source_target_pairs={{0,124},{1,125},{2,126},{3,127},{4,0},{5,1},{6,2},{7,3},{8,4},{9,5... | collective-permute-start | bytes 221192 | tf_op jit(solution)/shard_map/ppermute | solution.py:12
  18.0 37.2 %collective-permute-start.4 = (bf16[192,192]{1,0:T(8,128)(2,1)S(1)}, bf16[192,192]{1,0:T(8,128)(2,1)}, u32[]{:S(2)}, u32[]{:S(2)}) collective-permute-start(bf16[192,192]{1,0:T(8,128)(2,1)S(1)} %get-tuple-element.18), channel_id=1, source_target_pairs={{0,16},{1,17},{2,18},{3,19},{4,20},{5,21},{6,22},{7,23},{8,24},{9,... | collective-permute-start | bytes 221192 | tf_op jit(solution)/shard_map/ppermute | solution.py:12
  18.0 5.6 %copy-start.2 = (s32[4096]{0:T(1024)S(1)}, s32[4096]{0:T(1024)}, u32[]{:S(2)}) copy-start(s32[4096]{0:T(1024)} %param.7) | copy-start | bytes 49156
  18.0 7.4 %copy-start.16 = (s32[7]{0:T(128)S(1)}, s32[7]{0:T(128)}, u32[]{:S(2)}) copy-start(s32[7]{0:T(128)} %constant.125) | copy-start | bytes 88
  28.6 42.6 %copy-start.10 = (s32[26,7]{0,1:T(8,128)}, s32[26,7]{0,1:T(8,128)S(1)}, u32[]{:S(2)}) copy-start(s32[26,7]{0,1:T(8,128)S(1)} %copy.14) | copy-start | bytes 2188
  28.7 42.4 %copy-start.12 = (s32[2,14]{1,0:T(2,128)}, s32[2,14]{1,0:T(2,128)S(1)}, u32[]{:S(2)}) copy-start(s32[2,14]{1,0:T(2,128)S(1)} %copy.12) | copy-start | bytes 340
  34.1 8.6 %copy-start.8 = (s32[6,7]{1,0:T(8,128)}, s32[6,7]{1,0:T(8,128)S(1)}, u32[]{:S(2)}) copy-start(s32[6,7]{1,0:T(8,128)S(1)} %stack.75) | copy-start | bytes 508
  43.3 13.4 %collective-permute-start.5 = (bf16[192,192]{1,0:T(8,128)(2,1)S(1)}, bf16[192,192]{1,0:T(8,128)(2,1)S(1)}, u32[]{:S(2)}, u32[]{:S(2)}) collective-permute-start(bf16[192,192]{1,0:T(8,128)(2,1)S(1)} %get-tuple-element.17), channel_id=1, source_target_pairs={{0,112},{1,113},{2,114},{3,115},{4,116},{5,117},{6,118},{7,119},{8... | collective-permute-start | bytes 221192 | tf_op jit(solution)/shard_map/ppermute | solution.py:12
  99.3 18.5 %copy-start.4 = (bf16[26,192,192,1]{2,1,3,0:T(8,128)(2,1)S(1)}, bf16[26,192,192,1]{2,1,3,0:T(8,128)(2,1)}, u32[]{:S(2)}) copy-start(bf16[26,192,192,1]{2,1,3,0:T(8,128)(2,1)} %fusion.50) | copy-start | bytes 5750788
  102.9 105.7 %collective-permute-start.6 = (f32[192,7,192]{0,2,1:T(8,128)}, f32[192,7,192]{0,2,1:T(8,128)}, u32[]{:S(2)}, u32[]{:S(2)}) collective-permute-start(f32[192,7,192]{0,2,1:T(8,128)} %get-tuple-element.16), channel_id=1, source_target_pairs={{0,1},{1,2},{2,3},{3,4},{4,5},{5,6},{6,7},{7,8},{8,9},{9,10},{10,1... | collective-permute-start | bytes 3096584 | tf_op jit(solution)/shard_map/ppermute | solution.py:12
  102.9 114.0 %collective-permute-start.7 = (f32[192,7,192]{0,2,1:T(8,128)}, f32[192,7,192]{0,2,1:T(8,128)}, u32[]{:S(2)}, u32[]{:S(2)}) collective-permute-start(f32[192,7,192]{0,2,1:T(8,128)} %get-tuple-element.15), channel_id=1, source_target_pairs={{0,127},{1,0},{2,1},{3,2},{4,3},{5,4},{6,5},{7,6},{8,7},{9,8},{10,... | collective-permute-start | bytes 3096584 | tf_op jit(solution)/shard_map/ppermute | solution.py:12
  110.0 109.3 %collective-permute-start.8 = (f32[192,7,192]{0,2,1:T(8,128)}, f32[192,7,192]{0,2,1:T(8,128)}, u32[]{:S(2)}, u32[]{:S(2)}) collective-permute-start(f32[192,7,192]{0,2,1:T(8,128)} %get-tuple-element.14), channel_id=1, source_target_pairs={{0,4},{1,5},{2,6},{3,7},{4,8},{5,9},{6,10},{7,11},{8,12},{9,13},{1... | collective-permute-start | bytes 3096584 | tf_op jit(solution)/shard_map/ppermute | solution.py:12
  110.0 112.0 %collective-permute-start.9 = (f32[192,7,192]{0,2,1:T(8,128)}, f32[192,7,192]{0,2,1:T(8,128)}, u32[]{:S(2)}, u32[]{:S(2)}) collective-permute-start(f32[192,7,192]{0,2,1:T(8,128)} %get-tuple-element.13), channel_id=1, source_target_pairs={{0,124},{1,125},{2,126},{3,127},{4,0},{5,1},{6,2},{7,3},{8,4},{9,5... | collective-permute-start | bytes 3096584 | tf_op jit(solution)/shard_map/ppermute | solution.py:12
  117.8 106.8 %collective-permute-start.10 = (f32[192,7,192]{0,2,1:T(8,128)}, f32[192,7,192]{0,2,1:T(8,128)}, u32[]{:S(2)}, u32[]{:S(2)}) collective-permute-start(f32[192,7,192]{0,2,1:T(8,128)} %get-tuple-element.12), channel_id=1, source_target_pairs={{0,16},{1,17},{2,18},{3,19},{4,20},{5,21},{6,22},{7,23},{8,24},{9,... | collective-permute-start | bytes 3096584 | tf_op jit(solution)/shard_map/ppermute | solution.py:12
  135.8 46.4 %copy-start.6 = (s32[26,7,2,14]{0,3,1,2:T(8,128)S(1)}, s32[26,7,2,14]{0,3,1,2:T(8,128)}, u32[]{:S(2)}) copy-start(s32[26,7,2,14]{0,3,1,2:T(8,128)} %reduce_window_sum.22) | copy-start | bytes 61156
  135.8 46.4 %copy-start.11 = (s32[26,7]{0,1:T(8,128)S(1)}, s32[26,7]{0,1:T(8,128)}, u32[]{:S(2)}) copy-start(s32[26,7]{0,1:T(8,128)} %copy-done.10) | copy-start | bytes 2188
  135.8 46.4 %copy-start.13 = (s32[2,14]{1,0:T(2,128)S(1)}, s32[2,14]{1,0:T(2,128)}, u32[]{:S(2)}) copy-start(s32[2,14]{1,0:T(2,128)} %copy-done.12) | copy-start | bytes 340
  135.8 46.4 %copy-start.14 = (pred[26,2]{0,1:T(4,128)(4,1)S(1)}, pred[26,2]{0,1:T(4,128)(4,1)}, u32[]{:S(2)}) copy-start(pred[26,2]{0,1:T(4,128)(4,1)} %iota_compare_fusion.1) | copy-start | bytes 160
  182.1 26.5 %copy-start.5 = (f32[192,7,192]{0,2,1:T(8,128)S(1)}, f32[192,7,192]{0,2,1:T(8,128)}, u32[]{:S(2)}) copy-start(f32[192,7,192]{0,2,1:T(8,128)} %get-tuple-element.11) | copy-start | bytes 3096580
  208.6 27.7 %collective-permute-start.11 = (f32[192,7,192]{0,2,1:T(8,128)S(1)}, f32[192,7,192]{0,2,1:T(8,128)S(1)}, u32[]{:S(2)}, u32[]{:S(2)}) collective-permute-start(f32[192,7,192]{0,2,1:T(8,128)S(1)} %copy-done.5), channel_id=1, source_target_pairs={{0,112},{1,113},{2,114},{3,115},{4,116},{5,117},{6,118},{7,119},{8... | collective-permute-start | bytes 3096584 | tf_op jit(solution)/shard_map/ppermute | solution.py:12
  237.5 10.1 %copy-start.7 = (s32[6,7,2,14]{3,1,0,2:T(8,128)S(1)}, s32[6,7,2,14]{3,1,0,2:T(8,128)}, u32[]{:S(2)}) copy-start(s32[6,7,2,14]{3,1,0,2:T(8,128)} %reduce_window_sum.23) | copy-start | bytes 14116
  237.5 10.1 %copy-start.9 = (s32[6,7]{1,0:T(8,128)S(1)}, s32[6,7]{1,0:T(8,128)}, u32[]{:S(2)}) copy-start(s32[6,7]{1,0:T(8,128)} %copy-done.8) | copy-start | bytes 508
  237.5 10.1 %copy-start.15 = (pred[6,2]{0,1:T(4,128)(4,1)S(1)}, pred[6,2]{0,1:T(4,128)(4,1)}, u32[]{:S(2)}) copy-start(pred[6,2]{0,1:T(4,128)(4,1)} %iota_compare_fusion) | copy-start | bytes 40
  247.6 17.2 %copy-start.1 = (s32[256,14]{0,1:T(8,128)S(1)}, s32[256,14]{0,1:T(8,128)}, u32[]{:S(2)}) copy-start(s32[256,14]{0,1:T(8,128)} %param.8) | copy-start | bytes 43012
where the time goes:
time: 266 us; the launch traced here: 265 us
  local copies, waits for them, and re-layouts  121 us (45%)
  matrix products  84.1 us (32%)
  starting transfers between devices  42.2 us (16%)
  waiting for transfers between devices  9.24 us (3%)
  other arithmetic  7.62 us (3%)
    dot_general x2, local copies, waits for them, and re-layouts, per_device(): jnp.einsum('iba,ikbc->iakc', p_vals[6:], products[6:], preferred_element_...  48 us
    ppermute x12, starting transfers between devices, shifted(): lax.ppermute(value, axis, [(i, (i + by) % count) for i in range(count)])  42.2 us
    dot_general x2, matrix products, spread(): return jnp.einsum(form, weights, galerkin, precision=lax.Precision.HIGHEST)  38 us
    dot_general x1, matrix products, per_device(): jnp.einsum('ikab,ikbc->ikac', a_vals, gathered, preferred_element_type=jn...  24.8 us
    unnamed x45, local copies, waits for them, and re-layouts  24.6 us
    dot_general x1, matrix products, per_device(): jnp.einsum('iba,ikbc->iakc', p_vals[6:], products[6:], preferred_element_...  18 us
    gather x1, local copies, waits for them, and re-layouts, per_device(): gathered = prolong_pool[pool_index]  13.8 us
    another operation x2, local copies, waits for them, and re-layouts, per_device(): jnp.stack(received)  11.3 us
  transfers between devices with their start and end apart: 12, of which 1 were waited for; matrix products, arithmetic and copies ran while one was open for 52% of the time, Pallas kernels for 0%

commit v1 on v0

v1 whole, which is shorter than its diff:
```python
import jax
import jax.numpy as jnp
from jax import lax
from jax.experimental import pallas as pl
from jax.experimental.pallas import tpu as pltpu
from jax.sharding import PartitionSpec as P

OFFSETS = [0, 1, -1, 4, -4, 16, -16]
OPPOSITE = [0, 2, 1, 4, 3, 6, 5]
B = 192
RF = 32
RC = 2
KA = 7
KC = 14
FACES = 6
INNER = RF - FACES
REGIONS = 128
WINDOW = 128
ROWS = 2
F32 = jnp.float32
BF16 = jnp.bfloat16
MIB = 1024 * 1024


def dot(a, b):
    return lax.dot_general(a, b, (((1,), (0,)), ((), ())), preferred_element_type=F32)


def link_pairs(link):
    if link == 0:
        return [(d, d ^ 1) for d in range(REGIONS)]
    if link == 1:
        return [(d, (d + 1 if d % 2 else d - 1) % REGIONS) for d in range(REGIONS)]
    return [(d, (d + OFFSETS[link + 1]) % REGIONS) for d in range(REGIONS)]


def sent_face(link, core):
    return (1 + core, 2 - core)[link] if link < 2 else link + 1


def received_face(link, core):
    return (2 - core, 1 + core)[link] if link < 2 else link + 1


def sender_of(link, region, core):
    if link < 2:
        step = 1 - 2 * core if link == 0 else 2 * core - 1
    else:
        step = -OFFSETS[link + 1]
    return (region + step + REGIONS) % REGIONS


def mate_row(link, face):
    return 2 - face if link < 2 else OPPOSITE[face] - 1


def fill_slots(slot_ref, list_ref, region):
    for r in range(RC):
        for m in reversed(range(KC)):
            slot_ref[r, list_ref[m, region * RC + r]] = m


def face_kernel(region_ref, cols_ref, pcol_ref, a_hbm, p_hbm, o0, o1, o2, o3, o4, o5,
                a_ref, p_ref, sums_ref, rhs_ref, a_sem, p_sem):
    outs = (o0, o1, o2, o3, o4, o5)
    region = region_ref[0]
    core = region % 2
    first_row = region * RF
    base = first_row % WINDOW
    a_copies = [pltpu.make_async_copy(a_hbm.at[i], a_ref.at[i], a_sem.at[i]) for i in range(FACES)]
    p_copies = [pltpu.make_async_copy(p_hbm.at[pl.ds(8 * i, 8)], p_ref.at[pl.ds(8 * i, 8)], p_sem.at[i]) for i in range(4)]
    for c in p_copies:
        c.start()
    for c in a_copies:
        c.start()
    for c in p_copies:
        c.wait()
    for link in range(FACES):
        if link == 0:
            a_copies[0].wait()
            a_copies[1].wait()
        elif link > 1:
            a_copies[link].wait()
        face = sent_face(link, core)
        row = face - 1
        p_own = p_ref[row]
        sums_ref[...] = jnp.zeros_like(sums_ref)
        for k in range(1, KA - 1):
            slot = k + (k >= face) if link > 1 else k + (k >= face).astype(jnp.int32)
            column = cols_ref[slot, base + row]
            which = pcol_ref[column] - region * RC
            sums_ref[which] += dot(a_ref[row, slot], p_ref[column - first_row])
        rhs_ref[:, 0:B] = dot(a_ref[row, 0], p_own).astype(BF16)
        rhs_ref[:, B : 2 * B] = sums_ref[0].astype(BF16)
        rhs_ref[:, 2 * B : 3 * B] = sums_ref[1].astype(BF16)
        rhs_ref[:, 3 * B : 4 * B] = a_ref[row, face]
        outs[link][...] = dot(p_own.T, rhs_ref[...]).astype(BF16)


def inner_kernel(region_ref, cols_ref, pcol_ref, list_ref, a_ref, p_ref, out_ref, slot_ref):
    region = region_ref[0]
    first_row = region * RF
    base = first_row % WINDOW
    out_ref[...] = jnp.zeros_like(out_ref)
    fill_slots(slot_ref, list_ref, region)

    def step(i, carry):
        for s in range(ROWS):
            row = i * ROWS + s + FACES
            p_turned = p_ref[row].T
            r = pcol_ref[first_row + row] - region * RC
            columns = [cols_ref[k, base + row] for k in range(KA)]
            products = [dot(a_ref[row, k], p_ref[columns[k] - first_row]).astype(BF16) for k in range(KA)]
            for k in range(KA):
                out_ref[r, slot_ref[r, pcol_ref[columns[k]]]] += dot(p_turned, products[k])
        return carry

    lax.fori_loop(0, INNER // ROWS, step, 0)


def merge_kernel(region_ref, pcol_ref, list_ref, p_ref, m0, m1, m2, m3, m4, m5, acc_ref, out_hbm,
                 buf_ref, diag_ref, slot_ref, out_sem, rest_sem, diag_sem, cross_sem):
    msgs = (m0, m1, m2, m3, m4, m5)
    region = region_ref[0]
    core = region % 2
    first_row = region * RF
    fill_slots(slot_ref, list_ref, region)
    copies = []

    def send(source, r, m, sem):
        c = pltpu.make_async_copy(source, out_hbm.at[r, m], sem)
        c.start()
        copies.append(c)

    places = []
    for link in range(FACES):
        face = received_face(link, core)
        sender = sender_of(link, region, core)
        r = pcol_ref[sender * RF + face - 1] - region * RC
        mate = mate_row(link, face)
        which = pcol_ref[first_row + mate] - sender * RC
        spots = [slot_ref[r, sender * RC + h] for h in range(2)]
        places.append((r, spots, mate, which))
        for h in range(2):
            m = slot_ref[1 - r, sender * RC + h]
            send(acc_ref.at[1 - r, m], 1 - r, m, rest_sem.at[link, h])
    diag = [slot_ref[r, region * RC + r] for r in range(RC)]
    for r in range(RC):
        m = slot_ref[r, region * RC + 1 - r]
        send(acc_ref.at[r, m], r, m, cross_sem.at[r])
        diag_ref[r] = acc_ref[r, diag[r]]
    for link in range(FACES):
        r, spots, mate, which = places[link]
        msg = msgs[link]
        diag_ref[r] += msg[:, 0:B].astype(F32)
        for h in range(2):
            buf_ref[link, h] = acc_ref[r, spots[h]] + msg[:, (h + 1) * B : (h + 2) * B].astype(F32)
        buf_ref[link, which] += dot(msg[:, 3 * B : 4 * B], p_ref[mate])
        for h in range(2):
            send(buf_ref.at[link, h], r, spots[h], out_sem.at[link, h])
    for r in range(RC):
        send(diag_ref.at[r], r, diag[r], diag_sem.at[r])
    for c in copies:
        c.wait()


SMEM_ALL = pl.BlockSpec(memory_space=pltpu.SMEM)
VMEM_ALL = pl.BlockSpec(memory_space=pltpu.VMEM)
ANY_ALL = pl.BlockSpec(memory_space=pl.ANY)
COLS = pl.BlockSpec((KA, WINDOW), lambda i, g: (0, g[0] * RF // WINDOW), memory_space=pltpu.SMEM)
DMA = pltpu.SemaphoreType.DMA
SLOTS = pltpu.SMEM((RC, REGIONS * RC), jnp.int32)


def in_vmem(x):
    return pltpu.with_memory_space_constraint(x, pltpu.VMEM)


def in_hbm(x):
    return pltpu.with_memory_space_constraint(x, pltpu.HBM)


def per_device(a_cols, p_col, coarse_cols, a_vals, p_vals):
    region = lax.axis_index("parts").astype(jnp.int32).reshape(1)
    cols = a_cols.T
    listed = coarse_cols.T
    messages = pl.pallas_call(
        face_kernel,
        grid_spec=pltpu.PrefetchScalarGridSpec(
            num_scalar_prefetch=1,
            grid=(1,),
            in_specs=[COLS, SMEM_ALL, ANY_ALL, ANY_ALL],
            out_specs=[VMEM_ALL] * FACES,
            scratch_shapes=[
                pltpu.VMEM((FACES, KA, B, B), BF16),
                pltpu.VMEM((RF, B, B), BF16),
                pltpu.VMEM((2, B, B), F32),
                pltpu.VMEM((B, 4 * B), BF16),
                DMA((FACES,)),
                DMA((4,)),
            ],
        ),
        out_shape=[pltpu.VMEM((B, 4 * B), BF16)] * FACES,
        compiler_params=pltpu.CompilerParams(vmem_limit_bytes=14 * MIB),
        name="faces",
    )(region, cols, p_col, in_hbm(a_vals), in_hbm(p_vals))
    received = [None] * FACES
    for link in (0, 2, 3, 4, 5, 1):
        message = messages[link]
        if link == 1:
            message, received[0] = lax.optimization_barrier((message, received[0]))
        received[link] = lax.ppermute(message, "parts", link_pairs(link))
    inner = pl.pallas_call(
        inner_kernel,
        grid_spec=pltpu.PrefetchScalarGridSpec(
            num_scalar_prefetch=1,
            grid=(1,),
            in_specs=[COLS, SMEM_ALL, SMEM_ALL, VMEM_ALL, VMEM_ALL],
            out_specs=VMEM_ALL,
            scratch_shapes=[SLOTS],
        ),
        out_shape=pltpu.VMEM((RC, KC, B, B), F32),
        compiler_params=pltpu.CompilerParams(vmem_limit_bytes=4 * MIB),
        name="inner",
    )(region, cols, p_col, listed, in_vmem(a_vals), in_vmem(p_vals))
    return pl.pallas_call(
        merge_kernel,
        in_specs=[SMEM_ALL, SMEM_ALL, SMEM_ALL] + [VMEM_ALL] * 8,
        out_specs=ANY_ALL,
        out_shape=jax.ShapeDtypeStruct((RC, KC, B, B), F32),
        scratch_shapes=[
            pltpu.VMEM((FACES, 2, B, B), F32),
            pltpu.VMEM((RC, B, B), F32),
            SLOTS,
            DMA((FACES, 2)),
            DMA((FACES, 2)),
            DMA((RC,)),
            DMA((RC,)),
        ],
        compiler_params=pltpu.CompilerParams(vmem_limit_bytes=12 * MIB),
        name="merge",
    )(region, p_col, listed, in_vmem(p_vals), *[in_vmem(x) for x in received], in_vmem(inner))


def solution(mesh):
    placed = (P(), P(), P(), P("parts", None, None, None), P("parts", None, None))
    return jax.shard_map(
        per_device,
        mesh=mesh,
        in_specs=placed,
        out_specs=P("parts", None, None, None),
        check_vma=False,
    )
```

time: 266 us -> 48.2 us (0.18)
  the two profiles are of different devices: /device:TPU:0 before, /device:TPU:1 now
where the time goes in v1:
time: 48.2 us; the launch traced here: 48 us
  Pallas kernels  25.5 us (53%)
  starting transfers between devices  16.6 us (34%)
  waiting for transfers between devices  4.3 us (9%)
  local copies, waits for them, and re-layouts  1.64 us (3%)
    ppermute x6, starting transfers between devices, per_device(): received[link] = lax.ppermute(message, 'parts', link_pairs(link))  16.6 us
    pallas_call x1, Pallas kernels, per_device(): pl.pallas_call(inner_kernel, grid_spec=pltpu.PrefetchScalarGridSpec(num_s...  13.3 us
    pallas_call x1, Pallas kernels, per_device(): pl.pallas_call(face_kernel, grid_spec=pltpu.PrefetchScalarGridSpec(num_sc...  8.22 us
    ppermute x6, waiting for transfers between devices, per_device(): received[link] = lax.ppermute(message, 'parts', link_pairs(link))  4.3 us
    pallas_call x1, Pallas kernels, per_device(): pl.pallas_call(merge_kernel, in_specs=[SMEM_ALL, SMEM_ALL, SMEM_ALL] + [V...  3.91 us
    unnamed x12, local copies, waits for them, and re-layouts  1.64 us
  transfers between devices with their start and end apart: 6, of which 1 were waited for; matrix products, arithmetic and copies ran while one was open for 0% of the time, Pallas kernels for 28%

profile of v1, /device:TPU:1, one launch (start us, length us, event | category | flops | bytes accessed | tf_op | source)
XLA Modules:
  0.0 48.0 jit_solution(4356331755997184039)
XLA Ops:
  0.0 0.0 copy-start.2
  0.0 0.9 %copy-done.2 = s32[4096,7]{0,1:T(8,128)S(1)} copy-done((s32[4096,7]{0,1:T(8,128)S(1)}, s32[4096,7]{0,1:T(8,128)}, u32[]{:S(2)}) %copy-start.2) | copy-done | bytes 114712
  0.9 0.0 copy-start.3
  0.9 0.7 %copy-done.3 = s32[4096]{0:T(1024)S(1)} copy-done((s32[4096]{0:T(1024)S(1)}, s32[4096]{0:T(1024)}, u32[]{:S(2)}) %copy-start.3) | copy-done | bytes 16408
  1.6 0.0 copy-start
  1.6 0.0 copy-start.1
  1.6 0.0 copy-start.4
  1.6 0.0 copy-start.5
  1.6 8.2 %faces.1 = (bf16[192,768]{1,0:T(8,128)(2,1)S(1)}, bf16[192,768]{1,0:T(8,128)(2,1)S(1)}, bf16[192,768]{1,0:T(8,128)(2,1)S(1)}, bf16[192,768]{1,0:T(8,128)(2,1)S(1...) custom-call(s32[1]{0:T(128)} %bitcast.region_ref, s32[7,4096]{1,0:T(8,128)S(1)} %bitcast.3, ...), custom_call_target="tpu_custom_call" | custom-call | tf_op jit(solution)/shard_map/faces/pallas_call | solution.py:187
  9.9 1.5 %collective-permute-start = (bf16[192,768]{1,0:T(8,128)(2,1)S(1)}, bf16[192,768]{1,0:T(8,128)(2,1)S(1)}, u32[]{:S(2)}, u32[]{:S(2)}) collective-permute-start(bf16[192,768]{1,0:T(8,128)(2,1)S(1)} %get-tuple-element.14), channel_id=1, source_target_pairs={{0,1},{1,0},{2,3},{3,2},{4,5},{5,4},{6,7},{7,6},{8,9},{9,8},{10,11... | collective-permute-start | bytes 884744 | tf_op jit(solution)/shard_map/ppermute | solution.py:212
  11.4 2.9 %collective-permute-start.2 = (bf16[192,768]{1,0:T(8,128)(2,1)S(1)}, bf16[192,768]{1,0:T(8,128)(2,1)S(1)}, u32[]{:S(2)}, u32[]{:S(2)}) collective-permute-start(bf16[192,768]{1,0:T(8,128)(2,1)S(1)} %get-tuple-element.17), channel_id=1, source_target_pairs={{0,4},{1,5},{2,6},{3,7},{4,8},{5,9},{6,10},{7,11},{8,12},{9,13},{1... | collective-permute-start | bytes 884744 | tf_op jit(solution)/shard_map/ppermute | solution.py:212
  14.2 5.9 %collective-permute-start.3 = (bf16[192,768]{1,0:T(8,128)(2,1)S(1)}, bf16[192,768]{1,0:T(8,128)(2,1)S(1)}, u32[]{:S(2)}, u32[]{:S(2)}) collective-permute-start(bf16[192,768]{1,0:T(8,128)(2,1)S(1)} %get-tuple-element.18), channel_id=1, source_target_pairs={{0,124},{1,125},{2,126},{3,127},{4,0},{5,1},{6,2},{7,3},{8,4},{9,5... | collective-permute-start | bytes 884744 | tf_op jit(solution)/shard_map/ppermute | solution.py:212
  20.1 0.0 collective-permute-start.4
  20.1 5.1 %collective-permute-start.5 = (bf16[192,768]{1,0:T(8,128)(2,1)S(1)}, bf16[192,768]{1,0:T(8,128)(2,1)S(1)}, u32[]{:S(2)}, u32[]{:S(2)}) collective-permute-start(bf16[192,768]{1,0:T(8,128)(2,1)S(1)} %get-tuple-element.20), channel_id=1, source_target_pairs={{0,112},{1,113},{2,114},{3,115},{4,116},{5,117},{6,118},{7,119},{8... | collective-permute-start | bytes 884744 | tf_op jit(solution)/shard_map/ppermute | solution.py:212
  25.2 0.0 collective-permute-done.m0
  25.2 1.2 %collective-permute-start.1 = (bf16[192,768]{1,0:T(8,128)(2,1)S(1)}, bf16[192,768]{1,0:T(8,128)(2,1)S(1)}, u32[]{:S(2)}, u32[]{:S(2)}) collective-permute-start(bf16[192,768]{1,0:T(8,128)(2,1)S(1)} %get-tuple-element.16), channel_id=1, source_target_pairs={{0,127},{1,2},{2,1},{3,4},{4,3},{5,6},{6,5},{7,8},{8,7},{9,10},{10... | collective-permute-start | bytes 884744 | tf_op jit(solution)/shard_map/ppermute | solution.py:212
  26.4 0.0 copy-done
  26.4 0.0 copy-done.1
  26.4 0.0 copy-done.4
  26.4 0.0 copy-done.5
  26.4 13.3 %inner.1.acc_ref = f32[2,14,192,192]{3,2,1,0:T(8,128)S(1)} custom-call(s32[1]{0:T(128)} %bitcast.region_ref, s32[7,4096]{1,0:T(8,128)S(1)} %bitcast.4, s32[4096]{0:T(1024)S(1)} %copy-done.4, s32[14,256]{1,0:T(8,128)S(1)} %bitcast.5, bf16[32,7,192,192]{3,2,1,0:T(8,128)(2,1)S(1)} %copy-done, bf16[32,192,192]{2,1,0:T(8,128)(2,1)S(1)} %copy-done.1), custom_call_target="tpu_custom_call" | custom-call | tf_op jit(solution)/shard_map/inner/pallas_call | solution.py:213
  39.8 0.0 collective-permute-done.2.m2
  39.8 0.0 collective-permute-done.3.m3
  39.8 0.0 collective-permute-done.4.m4
  39.8 4.3 %collective-permute-done.5.m5 = bf16[192,768]{1,0:T(8,128)(2,1)S(1)} collective-permute-done((bf16[192,768]{1,0:T(8,128)(2,1)S(1)}, bf16[192,768]{1,0:T(8,128)(2,1)S(1)}, u32[]{:S(2)}, u32[]{:S(2)}) %collective-permute-start.5) | collective-permute-done | bytes 294944 | tf_op jit(solution)/shard_map/ppermute | solution.py:212
  44.1 0.0 collective-permute-done.1.m1
  44.1 3.9 %merge.1 = f32[2,14,192,192]{3,2,1,0:T(8,128)} custom-call(s32[1]{0:T(128)} %bitcast.region_ref, s32[4096]{0:T(1024)S(1)} %copy-done.4, s32[14,256]{1,0:T(8,128)S(1)} %bitcast.6, bf16[32,192,192]{2,1,0:T(8,128)(2,1)S(1)} %copy-done.1, bf16[192,768]{1,0:T(8,128)(2,1)S(1)} %collective-permute-done.m0, bf16[192,768]{1,0:T(8,128)(2,1)S(1)} %collective-permute-done.1.m1, ...), custom_call_target="tpu_custom_call" | custom-call | tf_op jit(solution)/shard_map/merge/pallas_call | solution.py:226
Async XLA Ops:
  0.0 0.9 %copy-start.2 = (s32[4096,7]{0,1:T(8,128)S(1)}, s32[4096,7]{0,1:T(8,128)}, u32[]{:S(2)}) copy-start(s32[4096,7]{0,1:T(8,128)} %param.5) | copy-start | bytes 344068
  0.9 0.7 %copy-start.3 = (s32[4096]{0:T(1024)S(1)}, s32[4096]{0:T(1024)}, u32[]{:S(2)}) copy-start(s32[4096]{0:T(1024)} %pcol_ref.5) | copy-start | bytes 49156
  1.6 24.8 %copy-start = (bf16[32,7,192,192]{3,2,1,0:T(8,128)(2,1)S(1)}, bf16[32,7,192,192]{3,2,1,0:T(8,128)(2,1)}, u32[]{:S(2)}) copy-start(bf16[32,7,192,192]{3,2,1,0:T(8,128)(2,1)} %a_ref.1) | copy-start | bytes 49545220
  1.6 24.8 %copy-start.1 = (bf16[32,192,192]{2,1,0:T(8,128)(2,1)S(1)}, bf16[32,192,192]{2,1,0:T(8,128)(2,1)}, u32[]{:S(2)}) copy-start(bf16[32,192,192]{2,1,0:T(8,128)(2,1)} %p_ref.3) | copy-start | bytes 7077892
  1.6 24.8 %copy-start.4 = (s32[4096]{0:T(1024)S(1)}, s32[4096]{0:T(1024)}, u32[]{:S(2)}) copy-start(s32[4096]{0:T(1024)} %pcol_ref.5) | copy-start | bytes 49156
  1.6 24.8 %copy-start.5 = (s32[256,14]{0,1:T(8,128)S(1)}, s32[256,14]{0,1:T(8,128)}, u32[]{:S(2)}) copy-start(s32[256,14]{0,1:T(8,128)} %param.7) | copy-start | bytes 43012
  9.9 15.4 %collective-permute-start = (bf16[192,768]{1,0:T(8,128)(2,1)S(1)}, bf16[192,768]{1,0:T(8,128)(2,1)S(1)}, u32[]{:S(2)}, u32[]{:S(2)}) collective-permute-start(bf16[192,768]{1,0:T(8,128)(2,1)S(1)} %get-tuple-element.14), channel_id=1, source_target_pairs={{0,1},{1,0},{2,3},{3,2},{4,5},{5,4},{6,7},{7,6},{8,9},{9,8},{10,11... | collective-permute-start | bytes 884744 | tf_op jit(solution)/shard_map/ppermute | solution.py:212
  11.4 28.4 %collective-permute-start.2 = (bf16[192,768]{1,0:T(8,128)(2,1)S(1)}, bf16[192,768]{1,0:T(8,128)(2,1)S(1)}, u32[]{:S(2)}, u32[]{:S(2)}) collective-permute-start(bf16[192,768]{1,0:T(8,128)(2,1)S(1)} %get-tuple-element.17), channel_id=1, source_target_pairs={{0,4},{1,5},{2,6},{3,7},{4,8},{5,9},{6,10},{7,11},{8,12},{9,13},{1... | collective-permute-start | bytes 884744 | tf_op jit(solution)/shard_map/ppermute | solution.py:212
  14.2 25.6 %collective-permute-start.3 = (bf16[192,768]{1,0:T(8,128)(2,1)S(1)}, bf16[192,768]{1,0:T(8,128)(2,1)S(1)}, u32[]{:S(2)}, u32[]{:S(2)}) collective-permute-start(bf16[192,768]{1,0:T(8,128)(2,1)S(1)} %get-tuple-element.18), channel_id=1, source_target_pairs={{0,124},{1,125},{2,126},{3,127},{4,0},{5,1},{6,2},{7,3},{8,4},{9,5... | collective-permute-start | bytes 884744 | tf_op jit(solution)/shard_map/ppermute | solution.py:212
  20.1 19.7 %collective-permute-start.4 = (bf16[192,768]{1,0:T(8,128)(2,1)S(1)}, bf16[192,768]{1,0:T(8,128)(2,1)S(1)}, u32[]{:S(2)}, u32[]{:S(2)}) collective-permute-start(bf16[192,768]{1,0:T(8,128)(2,1)S(1)} %get-tuple-element.19), channel_id=1, source_target_pairs={{0,16},{1,17},{2,18},{3,19},{4,20},{5,21},{6,22},{7,23},{8,24},{9,... | collective-permute-start | bytes 884744 | tf_op jit(solution)/shard_map/ppermute | solution.py:212
  20.1 24.0 %collective-permute-start.5 = (bf16[192,768]{1,0:T(8,128)(2,1)S(1)}, bf16[192,768]{1,0:T(8,128)(2,1)S(1)}, u32[]{:S(2)}, u32[]{:S(2)}) collective-permute-start(bf16[192,768]{1,0:T(8,128)(2,1)S(1)} %get-tuple-element.20), channel_id=1, source_target_pairs={{0,112},{1,113},{2,114},{3,115},{4,116},{5,117},{6,118},{7,119},{8... | collective-permute-start | bytes 884744 | tf_op jit(solution)/shard_map/ppermute | solution.py:212
  25.2 18.9 %collective-permute-start.1 = (bf16[192,768]{1,0:T(8,128)(2,1)S(1)}, bf16[192,768]{1,0:T(8,128)(2,1)S(1)}, u32[]{:S(2)}, u32[]{:S(2)}) collective-permute-start(bf16[192,768]{1,0:T(8,128)(2,1)S(1)} %get-tuple-element.16), channel_id=1, source_target_pairs={{0,127},{1,2},{2,1},{3,4},{4,3},{5,6},{6,5},{7,8},{8,7},{9,10},{10... | collective-permute-start | bytes 884744 | tf_op jit(solution)/shard_map/ppermute | solution.py:212
